TPU v7x, 128 devices: a whole 4x4x4 slice. The times are simulated.
128 devices in a mesh: sx: 8 (over z, core), sy: 16 (over y, x).
Axes of the slice: x: 4, y: 4, z: 4, core: 2. Of those that a mesh axis runs over, the one named last changes fastest.
Arguments:
- grid_points: float32 [3, 262144], P(None, ('sx', 'sy')), may hold values from 0 to 16
- weighted_density: float32 [262144], P(('sx', 'sy')), may hold values from -0.15 to 0.15
- point_slot: int32 [262144], P(('sx', 'sy')), may hold values from 0 to 127, as said below
- near_slot: int32 [2048, 64], P(('sx', 'sy')), may hold values from 0 to 127, as said below
- slot_atom: int32 [16384], replicated, may hold values from 0 to 2047, as said below
- atom_pos: float32 [3, 2048], replicated, may hold values from 0 to 16
- decay_rates: float32 [128], replicated, may hold values from 0.5 to 2
- green: float32 [7, 128, 128], replicated, may hold values from -0.5 to 0.5
- moment_table: float32 [3, 128], replicated, may hold values from 0.5 to 5
Outputs:
- potential: float32 [262144], P(('sx', 'sy'))
Inputs may be any that keep to these rules, and one draw needn't show every extreme that they name: `slot_atom`: atoms are owned in ranges in device order: devices below 32 own 2 * 16 atoms each, those below 64 own 16, the rest 16 // 2; the 128 atoms listed by one device are distinct; at most 2 of them have one owner, and in every draw one owner has exactly 2 atoms in every device's list. `near_slot`: the 64 entries of one batch are distinct. `point_slot`: each point's entry is one of its batch's near entries.
All inputs are finite; a program needn't handle non-finite values.
Results may differ from a plain program's by a relative error of at most 0.004.
Values may be sent and summed in bfloat16 or wider, within the bound.
A program may use at most 64 MiB of HBM per device.

v0:
```python
import math
import jax
import jax.numpy as jnp
import numpy as np
from jax import lax
from jax.sharding import PartitionSpec as P

HARM = 49
NRAD = 128
OWN_AVG = 16
OWN = 32


def harmonic_table(comp_x, comp_y, comp_z, top_degree):
    square = comp_x * comp_x + comp_y * comp_y + comp_z * comp_z
    cosines = [jnp.ones_like(comp_x)]
    sine_terms = [jnp.zeros_like(comp_x)]
    for m in range(1, top_degree + 1):
        cosines.append(cosines[m - 1] * comp_x - sine_terms[m - 1] * comp_y)
        sine_terms.append(cosines[m - 1] * comp_y + sine_terms[m - 1] * comp_x)
    legendre = {}
    for m in range(top_degree + 1):
        legendre[m, m] = float(math.prod(range(1, 2 * m, 2))) * cosines[0]
        if m + 1 <= top_degree:
            legendre[m + 1, m] = (2 * m + 1) * comp_z * legendre[m, m]
        for l in range(m + 2, top_degree + 1):
            legendre[l, m] = (
                (2 * l - 1) * comp_z * legendre[l - 1, m]
                - (l + m - 1) * square * legendre[l - 2, m]
            ) / (l - m)
    stacked = []
    for l in range(top_degree + 1):
        for m in range(l + 1):
            factor = math.sqrt(
                (2 * l + 1) / (4 * math.pi) * math.factorial(l - m) / math.factorial(l + m)
            )
            if m == 0:
                stacked.append(factor * legendre[l, 0])
            else:
                factor = factor * math.sqrt(2.0)
                stacked.append(factor * legendre[l, m] * cosines[m])
                stacked.append(factor * legendre[l, m] * sine_terms[m])
    return jnp.stack(stacked)


def soft_geometry(delta):
    distance = jnp.sqrt(jnp.sum(delta * delta, axis=0) + 1.0)
    return (distance, delta / distance)


def shell_layout(decay_rates):
    count = decay_rates.shape[0]
    spacing = 27.0 / (count - 1)
    centres = 1.0 + spacing * jnp.arange(count).astype(decay_rates.dtype)
    return (centres, spacing)


def shell_values(distance, rates, centres, spacing):
    offset = (distance - centres) / spacing
    return jnp.exp(-rates * offset * offset)


def project_points(points, density, slot_of_point, atom_list, atom_pos, decay_rates):
    listed = atom_list.shape[0]
    atom_ids = atom_list[slot_of_point]
    delta = points - atom_pos[:, atom_ids]
    distance, unit_vec = soft_geometry(delta)
    harmonics = harmonic_table(unit_vec[0], unit_vec[1], unit_vec[2], 6)
    projected = (density[None, :] * harmonics).astype(jnp.bfloat16)
    centres, spacing = shell_layout(decay_rates)
    radial = shell_values(
        distance[None, :], decay_rates[:, None], centres[:, None], spacing
    ).astype(jnp.bfloat16)
    onehot = (slot_of_point[None, :] == jnp.arange(listed)[:, None]).astype(jnp.bfloat16)
    weighted = onehot[:, None, :] * projected[None, :, :]
    terms = jnp.einsum("tip,kp->tik", weighted, radial, preferred_element_type=jnp.float32)
    return terms.reshape(listed, -1)


def apply_green(coefficients, green):
    pieces = []
    for l in range(7):
        pieces.append(
            jnp.einsum(
                "aik,kn->ain",
                coefficients[:, l * l : (l + 1) * (l + 1)],
                green[l],
                precision=lax.Precision.HIGHEST,
            )
        )
    return jnp.concatenate(pieces, axis=1)


def low_moments(coefficients, moment_table):
    degrees = np.array([0, 1, 1, 1, 2, 2, 2, 2, 2])
    table = moment_table[degrees]
    return jnp.einsum("aik,ik->ia", coefficients[:, :9], table, precision=lax.Precision.HIGHEST)


def near_field(points, near_ids, near_coef, atom_pos, decay_rates):
    batches = near_ids.shape[0]
    batch_pts = points.shape[1] // batches
    grouped = points.reshape(3, batches, batch_pts)
    delta = grouped[:, :, None, :] - atom_pos[:, near_ids][..., None]
    distance, unit_vec = soft_geometry(delta)
    harmonics = harmonic_table(unit_vec[0], unit_vec[1], unit_vec[2], 6)
    centres, spacing = shell_layout(decay_rates)
    radial = shell_values(
        distance[:, :, None, :],
        decay_rates[None, None, :, None],
        centres[None, None, :, None],
        spacing,
    ).astype(jnp.bfloat16)
    values = jnp.einsum("bjik,bjkp->bjip", near_coef, radial, preferred_element_type=jnp.float32)
    return jnp.sum(values * jnp.moveaxis(harmonics, 0, 2), axis=(1, 2)).reshape(-1)


def far_field(points, near_ids, moments, atom_pos):
    batches = near_ids.shape[0]
    batch_pts = points.shape[1] // batches
    grouped = jnp.moveaxis(points.reshape(3, batches, batch_pts), 1, 0)
    atom_index = jnp.arange(atom_pos.shape[1])

    def one_batch(inputs):
        coords, ids = inputs
        delta = coords[:, :, None] - atom_pos[:, None, :]
        distance, unit_vec = soft_geometry(delta)
        harmonics = harmonic_table(unit_vec[0], unit_vec[1], unit_vec[2], 2)
        inverse = 1.0 / distance
        keep = 1.0 - jnp.sum((ids[:, None] == atom_index[None, :]).astype(jnp.float32), axis=0)
        scaled = moments * keep[None, :]
        total = harmonics[0] * scaled[0][None, :] * inverse
        total = total + jnp.sum(harmonics[1:4] * scaled[1:4, None, :], axis=0) * inverse * inverse
        total = (
            total
            + jnp.sum(harmonics[4:9] * scaled[4:9, None, :], axis=0) * inverse * inverse * inverse
        )
        return jnp.sum(total, axis=1)

    return lax.map(one_batch, (grouped, near_ids)).reshape(-1)


def per_device(
    grid_points,
    weighted_density,
    point_slot,
    near_slot,
    slot_atom,
    atom_pos,
    decay_rates,
    green,
    moment_table,
):
    count_x = lax.axis_size("sx")
    count_y = lax.axis_size("sy")
    devices = count_x * count_y
    myself = lax.axis_index("sx") * count_y + lax.axis_index("sy")
    all_lists = slot_atom.reshape(devices, -1)
    listed = all_lists.shape[1]
    capacity = 2 * listed // devices
    total_atoms = atom_pos.shape[1]
    my_list = all_lists[myself]
    batches = near_slot.shape[0]
    near_count = near_slot.shape[1]
    batch_pts = grid_points.shape[1] // batches
    block = math.gcd(batches, 4)
    groups = batches // block
    group_points = jnp.moveaxis(grid_points.reshape(3, groups, block * batch_pts), 1, 0)
    group_density = weighted_density.reshape(groups, block * batch_pts)
    group_slots = point_slot.reshape(groups, block * batch_pts)
    group_near = near_slot.reshape(groups, block, near_count)
    width = HARM * NRAD

    def project_step(total, inputs):
        points, density, slot_of_point = inputs
        return (
            total + project_points(points, density, slot_of_point, my_list, atom_pos, decay_rates),
            None,
        )

    summed, unused = lax.scan(
        project_step,
        jnp.zeros((listed, width), jnp.float32),
        (group_points, group_density, group_slots),
    )
    partial_value = summed.astype(jnp.bfloat16)
    owner_ids = jnp.arange(devices)
    counts = jnp.where(
        owner_ids < devices // 4,
        2 * OWN_AVG,
        jnp.where(owner_ids < devices // 2, OWN_AVG, OWN_AVG // 2),
    ).astype(jnp.int32)
    range_ends = jnp.cumsum(counts)
    starts = range_ends - counts
    atom_index = jnp.arange(total_atoms)
    owner = jnp.sum((range_ends[None, :] <= atom_index[:, None]).astype(jnp.int32), axis=1)
    owners_all = owner[all_lists]
    my_dest = owners_all[myself]
    slot_index = jnp.arange(listed)
    same_owner = (my_dest[:, None] == my_dest[None, :]) & (
        slot_index[None, :] < slot_index[:, None]
    )
    earlier = jnp.sum(same_owner.astype(jnp.int32), axis=1)
    send_row = my_dest * capacity + earlier
    packing = (jnp.arange(devices * capacity)[:, None] == send_row[None, :]).astype(jnp.bfloat16)
    outgoing = jnp.dot(packing, partial_value, preferred_element_type=jnp.float32).astype(
        jnp.bfloat16
    )
    mine = owners_all == myself
    recv_rank = jnp.cumsum(mine.astype(jnp.int32), axis=1) - 1
    target = jnp.where(mine, owner_ids[:, None] * capacity + recv_rank, devices * capacity)
    local_ids = jnp.where(mine, all_lists - starts[myself], OWN)
    row_owned = (
        jnp.full((devices * capacity + 1,), OWN, jnp.int32)
        .at[target.reshape(-1)]
        .set(local_ids.reshape(-1))[: devices * capacity]
    )
    incoming = lax.all_to_all(outgoing, ("sx", "sy"), split_axis=0, concat_axis=0, tiled=True)
    selector = (row_owned[None, :] == jnp.arange(OWN)[:, None]).astype(jnp.bfloat16)
    coeff_own = jnp.dot(selector, incoming, preferred_element_type=jnp.float32).reshape(
        OWN, HARM, NRAD
    )
    pot_own = apply_green(coeff_own, green).astype(jnp.bfloat16).reshape(OWN, width)
    moments_own = low_moments(coeff_own, moment_table)
    reply = jnp.dot(selector.T, pot_own, preferred_element_type=jnp.float32).astype(jnp.bfloat16)
    returned = lax.all_to_all(reply, ("sx", "sy"), split_axis=0, concat_axis=0, tiled=True)
    gathered = lax.all_gather(moments_own, ("sx", "sy"), axis=1, tiled=True)
    column = owner * OWN + atom_index - starts[owner]
    moments_all = gathered[:, column]
    slot_pot = jnp.dot(packing.T, returned, preferred_element_type=jnp.float32).astype(jnp.bfloat16)
    near_ids = my_list[near_slot]
    group_ids = near_ids.reshape(groups, block, near_count)
    list_index = jnp.arange(listed)

    def near_group(inputs):
        points, ids, near_list = inputs
        picker = (near_list[:, :, None] == list_index[None, None, :]).astype(jnp.bfloat16)
        near_coef = jnp.einsum(
            "bjt,tw->bjw", picker, slot_pot, preferred_element_type=jnp.float32
        ).astype(jnp.bfloat16)
        near_coef = near_coef.reshape(block, near_count, HARM, NRAD)
        return near_field(points, ids, near_coef, atom_pos, decay_rates)

    near_part = lax.map(near_group, (group_points, group_ids, group_near)).reshape(-1)
    far_part = far_field(grid_points, near_ids, moments_all, atom_pos)
    return near_part + far_part


def solution(mesh):
    return jax.shard_map(
        per_device,
        mesh=mesh,
        in_specs=(
            P(None, ("sx", "sy")),
            P(("sx", "sy")),
            P(("sx", "sy")),
            P(("sx", "sy"), None),
            P(),
            P(),
            P(),
            P(),
            P(),
        ),
        out_specs=P(("sx", "sy")),
        check_vma=False,
    )
```

profile of v0, /device:TPU:0, one launch (start us, length us, event | category | flops | bytes accessed | tf_op | source)
XLA Modules:
  0.0 600.6 jit_solution(10263275687308145965)
XLA Ops:
  1.6 90.5 %gather_fusion.3 = s32[16384]{0:T(1024)S(1)} fusion(s32[2048]{0:T(1024)S(1)} %convert_reduce_fusion.1, s32[16384]{0:T(1024)S(1)} %fusion.58), kind=kCustom, calls=%fused_computation.3 | custom fusion | bytes 196608 | tf_op jit(solution)/shard_map/gather | solution.py:197
  96.2 83.5 %while.47 = (s32[]{:T(128)}, f32[128,6272]{0,1:T(8,128)S(1)}, s32[4,512]{1,0:T(4,128)S(1)}, f32[4,512]{1,0:T(4,128)}, f32[4,3,512]{2,1,0:T(4,128)}, /*index=5*/s...) while((s32[]{:T(128)}, f32[128,6272]{0,1:T(8,128)S(1)}, ...), condition=%wide.region_7.8_spmd.clone, body=%wide.region_5.7_spmd.clone.sunk | while | flops 827510272 | bytes 13908703 | solution.py:181
  96.8 3.3 gather_fusion.1
  105.4 2.9 stack.25
  109.7 4.5 fusion.142
  114.3 2.7 bitcast_add_fusion.4
  117.6 3.3 gather_fusion.1
  126.3 2.9 stack.25
  130.6 4.5 fusion.142
  135.1 2.7 bitcast_add_fusion.4
  138.5 3.3 gather_fusion.1
  147.1 2.9 stack.25
  151.4 4.5 fusion.142
  156.0 2.7 bitcast_add_fusion.4
  159.4 3.3 gather_fusion.1
  168.0 2.9 stack.25
  172.3 4.5 fusion.142
  176.9 2.7 bitcast_add_fusion.4
  179.6 3.3 convolution_convert_fusion.2
  183.0 7.2 %all_to_all.16 = bf16[128,2,6272]{2,1,0:T(2,128)(2,1)} reshape(bf16[256,6272]{1,0:T(8,128)(2,1)} %convolution_convert_fusion.2) | data formatting | bytes 6422528 | tf_op jit(solution)/shard_map/all_to_all | solution.py:218
  190.1 11.6 %all-to-all-start = ((bf16[128,2,6272]{2,1,0:T(2,128)(2,1)}), bf16[128,2,6272]{2,1,0:T(2,128)(2,1)}, u32[]{:S(2)}, u32[]{:S(2)}) async-start(bf16[128,2,6272]{2,1,0:T(2,128)(2,1)} %all_to_all.16), calls=%async_computation | async-start | bytes 6422528 | tf_op jit(solution)/shard_map/all_to_all | solution.py:218
  202.5 6.6 %gather_fusion.4 = s32[1024]{0:T(1024)S(1)} fusion(s32[128]{0:T(128)S(1)} %get-tuple-element.1387, s32[1024]{0:T(1024)S(1)} %get-tuple-element.976), kind=kCustom, calls=%fused_computation.4 | custom fusion | bytes 12288 | tf_op jit(solution)/shard_map/gather | solution.py:231
  210.5 60.5 %scatter_custom_fusion = s32[257]{0:T(512)S(1)} fusion(s32[16384]{0:T(1024)S(1)} %bitcast.236, s32[16384]{0:T(1024)S(1)} %subtract_select_fusion, s32[]{:T(128)} %constant.1003.clone.1), kind=kCustom, calls=%fused_computation.317 | custom fusion | bytes 1032 | tf_op jit(solution)/shard_map/scatter | solution.py:216
  271.0 12.6 %gather_fusion.6 = s32[2048]{0:T(1024)S(1)} fusion(s32[128]{0:T(128)S(1)} %fusion.85, s32[2048]{0:T(1024)S(1)} %broadcast_clamp_fusion.1), kind=kCustom, calls=%fused_computation.6 | custom fusion | bytes 24576 | tf_op jit(solution)/shard_map/gather | solution.py:228
  284.3 6.3 %all_to_all.18 = bf16[256,6272]{1,0:T(8,128)(2,1)S(1)} reshape(bf16[128,2,6272]{2,1,0:T(2,128)(2,1)} %all-to-all-done) | data formatting | bytes 6422528 | tf_op jit(solution)/shard_map/all_to_all | solution.py:218
  290.5 3.5 copy.274
  294.0 2.9 fusion.77
  305.8 2.8 all_to_all.19
  308.6 9.7 %all-to-all-start.1 = ((bf16[128,2,6272]{2,1,0:T(2,128)(2,1)}), bf16[128,2,6272]{2,1,0:T(2,128)(2,1)S(1)}, u32[]{:S(2)}, u32[]{:S(2)}) async-start(bf16[128,2,6272]{2,1,0:T(2,128)(2,1)} %all_to_all.19), calls=%async_computation.1 | async-start | bytes 6422528 | tf_op jit(solution)/shard_map/all_to_all | solution.py:226
  319.5 94.5 %all-gather = f32[128,32,9]{1,2,0:T(8,128)} all-gather(f32[1,32,9]{1,2,0:T(8,128)S(1)} %bitcast.239), channel_id=1, replica_groups=mesh['sx'=8,'sy'=16] {'sx','sy'}, dimensions={0}, use_global_device_ids=true | all-gather | bytes 148608 | tf_op jit(solution)/shard_map/all_gather | solution.py:227
  414.0 3.4 copy.277
  417.4 9.2 %gather_fusion.7 = f32[2048,9]{1,0:T(8,128)} fusion(f32[9,4096]{0,1:T(8,128)} %bitcast.216, s32[2048]{0:T(1024)S(1)} %broadcast_clamp_fusion), kind=kCustom, calls=%fused_computation.7 | custom fusion | bytes 155648 | tf_op jit(solution)/shard_map/gather | solution.py:229
  428.1 72.1 %while.46 = (s32[]{:T(128)}, f32[16,128]{1,0:T(8,128)S(1)}, f32[16,3,128]{2,1,0:T(4,128)S(1)}, f32[3,2048]{1,0:T(4,128)S(1)}, s32[16,64]{1,0:T(8,128)S(1)}, /*index=5*/f32[9,2048]{1,0:T(8,128)S(1)}, s32[]{:T(128)}, s32[]{:T(128)}) while((s32[]{:T(128)}, f32[16,128]{1,0:T(8,128)S(1)}, f32[16,3,128]{2,1,0:T(4,128)S(1)}, ...), condition=%wide.region_18.19_spmd.clone, body=%wide.region_12.18_spmd.clone.sunk | while | flops 21122944 | bytes 44499296 | solution.py:140
  500.2 2.8 all_to_all.21
  503.0 3.7 convolution_convert_fusion.3
  506.7 93.2 %while.45 = (s32[]{:T(128)}, f32[4,512]{1,0:T(4,128)S(1)}, s32[4,4,64]{2,1,0:T(4,128)S(1)}, bf16[128,6272]{1,0:T(8,128)(2,1)}, f32[4,3,512]{2,1,0:T(4,128)S(1)},...) while((s32[]{:T(128)}, f32[4,512]{1,0:T(4,128)S(1)}, ...), condition=%wide.region_11.12_spmd.clone, body=%wide.region_8.11_spmd.clone.sunk | while | flops 861898496 | bytes 92647080 | solution.py:244
  515.7 3.1 reshape.986
  518.7 6.9 %fusion.129 = f32[4,64,49,128]{3,2,1,0:T(8,128)S(1)} fusion(bf16[4,64,49,128]{3,2,1,0:T(8,128)(2,1)} %reshape.986, f32[128]{0:T(128)S(1)} %multiply_bitcast_fusion.4, f32[128]{0:T(128)S(1)} %multiply_add_fusion.29, f32[4,64,128]{2,1,0:T(8,128)S(1)} %add_sqrt_fusion.6), kind=kOutput, calls=%fused_computation.17.clone.1 | convolution fusion | flops 432013312 | bytes 9765888 | tf_op jit(solution)/shard_map/while/body/eval_jaxpr/bjik,bjkp->bjip/dot_general | solution.py:114
  525.7 4.3 fusion.130
  539.0 3.1 reshape.986
  542.0 6.9 %fusion.129 = f32[4,64,49,128]{3,2,1,0:T(8,128)S(1)} fusion(bf16[4,64,49,128]{3,2,1,0:T(8,128)(2,1)} %reshape.986, f32[128]{0:T(128)S(1)} %multiply_bitcast_fusion.4, f32[128]{0:T(128)S(1)} %multiply_add_fusion.29, f32[4,64,128]{2,1,0:T(8,128)S(1)} %add_sqrt_fusion.6), kind=kOutput, calls=%fused_computation.17.clone.1 | convolution fusion | flops 432013312 | bytes 9765888 | tf_op jit(solution)/shard_map/while/body/eval_jaxpr/bjik,bjkp->bjip/dot_general | solution.py:114
  549.0 4.3 fusion.130
  562.3 3.1 reshape.986
  565.4 6.9 %fusion.129 = f32[4,64,49,128]{3,2,1,0:T(8,128)S(1)} fusion(bf16[4,64,49,128]{3,2,1,0:T(8,128)(2,1)} %reshape.986, f32[128]{0:T(128)S(1)} %multiply_bitcast_fusion.4, f32[128]{0:T(128)S(1)} %multiply_add_fusion.29, f32[4,64,128]{2,1,0:T(8,128)S(1)} %add_sqrt_fusion.6), kind=kOutput, calls=%fused_computation.17.clone.1 | convolution fusion | flops 432013312 | bytes 9765888 | tf_op jit(solution)/shard_map/while/body/eval_jaxpr/bjik,bjkp->bjip/dot_general | solution.py:114
  572.3 4.3 fusion.130
  585.6 3.1 reshape.986
  588.7 6.9 %fusion.129 = f32[4,64,49,128]{3,2,1,0:T(8,128)S(1)} fusion(bf16[4,64,49,128]{3,2,1,0:T(8,128)(2,1)} %reshape.986, f32[128]{0:T(128)S(1)} %multiply_bitcast_fusion.4, f32[128]{0:T(128)S(1)} %multiply_add_fusion.29, f32[4,64,128]{2,1,0:T(8,128)S(1)} %add_sqrt_fusion.6), kind=kOutput, calls=%fused_computation.17.clone.1 | convolution fusion | flops 432013312 | bytes 9765888 | tf_op jit(solution)/shard_map/while/body/eval_jaxpr/bjik,bjkp->bjip/dot_general | solution.py:114
  595.6 4.3 fusion.130
  (802 shorter events, 153.0 us)
Async XLA Ops:
  0.0 283.6 %copy-start = (f32[3,128]{1,0:T(4,128)S(1)}, f32[3,128]{1,0:T(4,128)}, u32[]{:S(2)}) copy-start(f32[3,128]{1,0:T(4,128)} %param.25) | copy-start | bytes 4612
  0.3 91.8 %copy-start.17 = (s32[128]{0:T(128)}, s32[128]{0:T(128)S(1)}, u32[]{:S(2)}) copy-start(s32[128]{0:T(128)S(1)} %reduce) | copy-start | bytes 1540
  1.5 90.8 %copy-start.5 = (f32[3,2048]{1,0:T(4,128)S(1)}, f32[3,2048]{1,0:T(4,128)}, u32[]{:S(2)}) copy-start(f32[3,2048]{1,0:T(4,128)} %param.22) | copy-start | bytes 73732
  1.5 92.2 %copy-start.20 = (f32[128]{0:T(128)S(1)}, f32[128]{0:T(128)}, u32[]{:S(2)}) copy-start(f32[128]{0:T(128)} %param.23) | copy-start | bytes 1540
  1.5 92.8 %copy-start.14 = (s32[2048]{0:T(1024)S(1)}, s32[2048]{0:T(1024)}, u32[]{:S(2)}) copy-start(s32[2048]{0:T(1024)} %param.19) | copy-start | bytes 24580
  1.6 92.8 %copy-start.15 = (f32[2048]{0:T(1024)S(1)}, f32[2048]{0:T(1024)}, u32[]{:S(2)}) copy-start(f32[2048]{0:T(1024)} %param.18) | copy-start | bytes 24580
  92.1 4.0 copy-start.8
  96.2 0.6 copy-start.12
  103.3 0.6 copy-start.10
  114.3 2.8 copy-start.13
  117.0 0.6 copy-start.12
  124.1 0.6 copy-start.10
  135.1 2.8 copy-start.13
  137.9 0.6 copy-start.12
  145.0 0.6 copy-start.10
  156.0 2.8 copy-start.13
  158.8 0.6 copy-start.12
  165.9 0.6 copy-start.10
  176.9 2.8 copy-start.13
  183.0 18.8 %copy-start.9 = (s32[16384]{0:T(1024)S(1)}, s32[16384]{0:T(1024)}, u32[]{:S(2)}) copy-start(s32[16384]{0:T(1024)} %copy-done.8) | copy-start | bytes 196612
  183.0 19.4 %copy-start.11 = (s32[16,64]{1,0:T(8,128)S(1)}, s32[16,64]{1,0:T(8,128)}, u32[]{:S(2)}) copy-start(s32[16,64]{1,0:T(8,128)} %param.20) | copy-start | bytes 12292
  183.0 19.5 %copy-start.19 = (s32[9]{0:T(128)S(1)}, s32[9]{0:T(128)}, u32[]{:S(2)}) copy-start(s32[9]{0:T(128)} %constant.1017) | copy-start | bytes 112
  190.1 19.1 %copy-start.18 = (s32[128]{0:T(128)S(1)}, s32[128]{0:T(128)}, u32[]{:S(2)}) copy-start(s32[128]{0:T(128)} %copy-done.17) | copy-start | bytes 1540
  190.1 19.7 %copy-start.7 = (s32[16384]{0:T(1024)S(1)}, s32[16384]{0:T(1024)}, u32[]{:S(2)}) copy-start(s32[16384]{0:T(1024)} %param.21) | copy-start | bytes 196612
  190.1 94.1 %all-to-all-start = ((bf16[128,2,6272]{2,1,0:T(2,128)(2,1)}), bf16[128,2,6272]{2,1,0:T(2,128)(2,1)}, u32[]{:S(2)}, u32[]{:S(2)}) async-start(bf16[128,2,6272]{2,1,0:T(2,128)(2,1)} %all_to_all.16), calls=%async_computation | async-start | bytes 6422528 | tf_op jit(solution)/shard_map/all_to_all | solution.py:218
  296.9 6.6 %copy-start.4 = (f32[32,49,128]{2,0,1:T(8,128)}, f32[32,49,128]{2,0,1:T(8,128)S(1)}, u32[]{:S(2)}) copy-start(f32[32,49,128]{2,0,1:T(8,128)S(1)} %fusion.77) | copy-start | bytes 2408452
  308.6 119.6 %copy-start.6 = (f32[4,3,512]{2,1,0:T(4,128)S(1)}, f32[4,3,512]{2,1,0:T(4,128)}, u32[]{:S(2)}) copy-start(f32[4,3,512]{2,1,0:T(4,128)} %get-tuple-element.1392) | copy-start | bytes 73732
  308.6 191.7 %all-to-all-start.1 = ((bf16[128,2,6272]{2,1,0:T(2,128)(2,1)}), bf16[128,2,6272]{2,1,0:T(2,128)(2,1)S(1)}, u32[]{:S(2)}, u32[]{:S(2)}) async-start(bf16[128,2,6272]{2,1,0:T(2,128)(2,1)} %all_to_all.19), calls=%async_computation.1 | async-start | bytes 6422528 | tf_op jit(solution)/shard_map/all_to_all | solution.py:226
  500.2 2.8 copy-start.16
  500.2 6.5 %copy-start.21 = (f32[1,1,128,1]{2,3,1,0:T(1,128)S(1)}, f32[1,1,128,1]{2,3,1,0:T(1,128)}, u32[]{:S(2)}) copy-start(f32[1,1,128,1]{2,3,1,0:T(1,128)} %get-tuple-element.1340) | copy-start | bytes 1540
  510.3 4.3 copy-start.3
  511.9 2.7 copy-start.2
  533.6 4.3 copy-start.3
  535.2 2.7 copy-start.2
  556.9 4.3 copy-start.3
  558.5 2.7 copy-start.2
  580.2 4.3 copy-start.3
  581.8 2.7 copy-start.2
  599.9 0.7 copy-start.1
where the time goes:
time: 604 us; the launch traced here: 601 us
  local copies, waits for them, and re-layouts  286 us (47%)
  other arithmetic  124 us (21%)
  blocking collectives  94.5 us (16%)
  matrix products  70.1 us (12%)
  starting transfers between devices  21.3 us (4%)
    all_gather x1, blocking collectives, per_device(): gathered = lax.all_gather(moments_own, ('sx', 'sy'), axis=1, tiled=True)  94.5 us
    gather x2, local copies, waits for them, and re-layouts, per_device(): owners_all = owner[all_lists]  90.6 us
    scatter x1, local copies, waits for them, and re-layouts, per_device(): row_owned = jnp.full((devices * capacity + 1,), OWN, jnp.int32).at[target...  60.5 us
    dot_general x4, matrix products, near_field(): jnp.einsum('bjik,bjkp->bjip', near_coef, radial, preferred_element_type=j...  27.8 us
    while x236, other arithmetic  21 us
    dot_general x4, matrix products, project_points(): jnp.einsum('tip,kp->tik', weighted, radial, preferred_element_type=jnp.fl...  18.2 us
    reduce_sum x4, other arithmetic, near_field(): jnp.sum(values * jnp.moveaxis(harmonics, 0, 2), axis=(1, 2)).reshape(-1)  17.1 us
    all_to_all x3, local copies, waits for them, and re-layouts, per_device(): lax.all_to_all(outgoing, ('sx', 'sy'), split_axis=0, concat_axis=0, tiled...  16.9 us
  transfers between devices with their start and end apart: 2, of which 0 were waited for; matrix products, arithmetic and copies ran while one was open for 28% of the time, Pallas kernels for 0%

commit v1 on v0

--- a/solution.py
+++ b/solution.py
@@ -4,6 +4,7 @@
 import numpy as np
 from jax import lax
 from jax.sharding import PartitionSpec as P
+from jax.lax import all_to_all, axis_size
 
 HARM = 49
 NRAD = 128
@@ -224,7 +225,10 @@
     moments_own = low_moments(coeff_own, moment_table)
     reply = jnp.dot(selector.T, pot_own, preferred_element_type=jnp.float32).astype(jnp.bfloat16)
     returned = lax.all_to_all(reply, ("sx", "sy"), split_axis=0, concat_axis=0, tiled=True)
-    gathered = lax.all_gather(moments_own, ("sx", "sy"), axis=1, tiled=True)
+    write_packet_all = lambda vals: jnp.concatenate(
+        all_to_all(jnp.stack(axis_size(("sx", "sy")) * [vals]), ("sx", "sy"), 0, 0), axis=1
+    )
+    gathered = write_packet_all(moments_own)
     column = owner * OWN + atom_index - starts[owner]
     moments_all = gathered[:, column]
     slot_pot = jnp.dot(packing.T, returned, preferred_element_type=jnp.float32).astype(jnp.bfloat16)

time: 604 us -> 517 us (0.86)
  blocking collectives: 94.5 us -> 0 us
    all_gather x1 -> x0, blocking collectives: 94.5 us -> none  [per_device(): gathered = lax.all_gather(moments_own, ('sx', 'sy'), axis=1, tiled=True)]
    all_to_all x0 -> x1, starting transfers between devices: none -> 9.69 us  [per_device(): all_to_all(jnp.stack(axis_size(('sx', 'sy')) * [vals]), ('sx', 'sy'), 0, 0)]
  transfers between devices with their start and end apart: 2 -> 3, of which waited for: 0 -> 1; matrix products, arithmetic and copies ran while one was open for 28% -> 31% of each run, Pallas kernels for 0% -> 0%
where the time goes in v1:
time: 517 us; the launch traced here: 515 us
  local copies, waits for them, and re-layouts  284 us (55%)
  other arithmetic  124 us (24%)
  matrix products  68.3 us (13%)
  starting transfers between devices  27.3 us (5%)
  waiting for transfers between devices  5.41 us (1%)
    gather x2, local copies, waits for them, and re-layouts, per_device(): owners_all = owner[all_lists]  90.6 us
    scatter x1, local copies, waits for them, and re-layouts, per_device(): row_owned = jnp.full((devices * capacity + 1,), OWN, jnp.int32).at[target...  60.5 us
    dot_general x4, matrix products, near_field(): jnp.einsum('bjik,bjkp->bjip', near_coef, radial, preferred_element_type=j...  27.7 us
    while x236, other arithmetic  21 us
    dot_general x4, matrix products, project_points(): jnp.einsum('tip,kp->tik', weighted, radial, preferred_element_type=jnp.fl...  18.3 us
    reduce_sum x4, other arithmetic, near_field(): jnp.sum(values * jnp.moveaxis(harmonics, 0, 2), axis=(1, 2)).reshape(-1)  17.1 us
    all_to_all x3, local copies, waits for them, and re-layouts, per_device(): lax.all_to_all(outgoing, ('sx', 'sy'), split_axis=0, concat_axis=0, tiled...  16.9 us
    while x44, local copies, waits for them, and re-layouts  15.4 us
  transfers between devices with their start and end apart: 3, of which 1 were waited for; matrix products, arithmetic and copies ran while one was open for 31% of the time, Pallas kernels for 0%

profile of v1, /device:TPU:0, one launch (start us, length us, event | category | flops | bytes accessed | tf_op | source)
XLA Modules:
  0.0 514.5 jit_solution(2953137239152245123)
XLA Ops:
  1.6 90.5 %gather_fusion.3 = s32[16384]{0:T(1024)S(1)} fusion(s32[2048]{0:T(1024)S(1)} %convert_reduce_fusion.1, s32[16384]{0:T(1024)S(1)} %fusion.58), kind=kCustom, calls=%fused_computation.3 | custom fusion | bytes 196608 | tf_op jit(solution)/shard_map/gather | solution.py:198
  96.1 83.7 %while.47 = (s32[]{:T(128)}, f32[128,6272]{0,1:T(8,128)S(1)}, s32[4,512]{1,0:T(4,128)S(1)}, f32[4,512]{1,0:T(4,128)}, f32[4,3,512]{2,1,0:T(4,128)}, /*index=5*/s...) while((s32[]{:T(128)}, f32[128,6272]{0,1:T(8,128)S(1)}, ...), condition=%wide.region_7.8_spmd.clone, body=%wide.region_5.7_spmd.clone.sunk | while | flops 827510272 | bytes 13908703 | solution.py:182
  96.7 3.3 gather_fusion.1
  105.4 2.9 stack.28
  109.7 4.6 fusion.142
  114.3 2.7 bitcast_add_fusion.4
  117.7 3.3 gather_fusion.1
  126.3 2.9 stack.28
  130.6 4.6 fusion.142
  135.2 2.7 bitcast_add_fusion.4
  138.6 3.3 gather_fusion.1
  147.2 2.9 stack.28
  151.6 4.6 fusion.142
  156.1 2.7 bitcast_add_fusion.4
  159.5 3.3 gather_fusion.1
  168.2 2.9 stack.28
  172.5 4.6 fusion.142
  177.1 2.7 bitcast_add_fusion.4
  179.8 3.3 convolution_convert_fusion.2
  183.2 7.2 %all_to_all.19 = bf16[128,2,6272]{2,1,0:T(2,128)(2,1)} reshape(bf16[256,6272]{1,0:T(8,128)(2,1)} %convolution_convert_fusion.2) | data formatting | bytes 6422528 | tf_op jit(solution)/shard_map/all_to_all | solution.py:219
  190.3 11.6 %all-to-all-start = ((bf16[128,2,6272]{2,1,0:T(2,128)(2,1)}), bf16[128,2,6272]{2,1,0:T(2,128)(2,1)}, u32[]{:S(2)}, u32[]{:S(2)}) async-start(bf16[128,2,6272]{2,1,0:T(2,128)(2,1)} %all_to_all.19), calls=%async_computation | async-start | bytes 6422528 | tf_op jit(solution)/shard_map/all_to_all | solution.py:219
  202.7 6.6 %gather_fusion.4 = s32[1024]{0:T(1024)S(1)} fusion(s32[128]{0:T(128)S(1)} %get-tuple-element.1387, s32[1024]{0:T(1024)S(1)} %get-tuple-element.976), kind=kCustom, calls=%fused_computation.4 | custom fusion | bytes 12288 | tf_op jit(solution)/shard_map/gather | solution.py:235
  210.7 60.5 %scatter_custom_fusion = s32[257]{0:T(512)S(1)} fusion(s32[16384]{0:T(1024)S(1)} %bitcast.232, s32[16384]{0:T(1024)S(1)} %subtract_select_fusion, s32[]{:T(128)} %constant.1003.clone.1), kind=kCustom, calls=%fused_computation.317 | custom fusion | bytes 1032 | tf_op jit(solution)/shard_map/scatter | solution.py:217
  271.2 12.6 %gather_fusion.6 = s32[2048]{0:T(1024)S(1)} fusion(s32[128]{0:T(128)S(1)} %fusion.85, s32[2048]{0:T(1024)S(1)} %broadcast_clamp_fusion.1), kind=kCustom, calls=%fused_computation.6 | custom fusion | bytes 24576 | tf_op jit(solution)/shard_map/gather | solution.py:232
  284.5 6.3 %all_to_all.21 = bf16[256,6272]{1,0:T(8,128)(2,1)S(1)} reshape(bf16[128,2,6272]{2,1,0:T(2,128)(2,1)} %all-to-all-done) | data formatting | bytes 6422528 | tf_op jit(solution)/shard_map/all_to_all | solution.py:219
  290.7 3.5 copy.274
  294.2 2.9 fusion.77
  306.9 9.7 %all-to-all-start.2 = ((f32[128,1,288]{2,1,0:T(1,128)}), f32[128,1,288]{2,1,0:T(1,128)S(1)}, u32[]{:S(2)}, u32[]{:S(2)}) async-start(f32[128,1,288]{2,1,0:T(1,128)} %reshape.983), calls=%async_computation.2 | async-start | bytes 393216 | tf_op jit(solution)/shard_map/all_to_all | solution.py:229
  318.6 2.8 all_to_all.22
  321.4 5.4 %all-to-all-done.2 = f32[128,1,288]{2,1,0:T(1,128)S(1)} async-done(((f32[128,1,288]{2,1,0:T(1,128)}), f32[128,1,288]{2,1,0:T(1,128)S(1)}, u32[]{:S(2)}, u32[]{:S(2)}) %all-to-all-start.2) | async-done | bytes 147488 | tf_op jit(solution)/shard_map/all_to_all | solution.py:229
  326.8 6.0 %all-to-all-start.1 = ((bf16[128,2,6272]{2,1,0:T(2,128)(2,1)}), bf16[128,2,6272]{2,1,0:T(2,128)(2,1)}, u32[]{:S(2)}, u32[]{:S(2)}) async-start(bf16[128,2,6272]{2,1,0:T(2,128)(2,1)} %all_to_all.22), calls=%async_computation.1 | async-start | bytes 6422528 | tf_op jit(solution)/shard_map/all_to_all | solution.py:227
  336.4 5.5 %gather_fusion.7 = f32[2048,9]{1,0:T(8,128)S(1)} fusion(f32[9,4096]{0,1:T(8,128)S(1)} %bitcast.211, s32[2048]{0:T(1024)S(1)} %broadcast_clamp_fusion), kind=kCustom, calls=%fused_computation.7 | custom fusion | bytes 155648 | tf_op jit(solution)/shard_map/gather | solution.py:233
  342.2 70.3 %while.46 = (s32[]{:T(128)}, f32[16,128]{1,0:T(8,128)S(1)}, f32[16,3,128]{2,1,0:T(4,128)S(1)}, f32[3,2048]{1,0:T(4,128)S(1)}, s32[16,64]{1,0:T(8,128)S(1)}, /*index=5*/f32[9,2048]{1,0:T(8,128)S(1)}, s32[]{:T(128)}, s32[]{:T(128)}) while((s32[]{:T(128)}, f32[16,128]{1,0:T(8,128)S(1)}, f32[16,3,128]{2,1,0:T(4,128)S(1)}, ...), condition=%wide.region_18.19_spmd.clone, body=%wide.region_12.18_spmd.clone.sunk | while | flops 21122944 | bytes 44499296 | solution.py:141
  412.5 6.3 %all_to_all.24 = bf16[256,6272]{1,0:T(8,128)(2,1)S(1)} reshape(bf16[128,2,6272]{2,1,0:T(2,128)(2,1)} %all-to-all-done.1) | data formatting | bytes 6422528 | tf_op jit(solution)/shard_map/all_to_all | solution.py:227
  420.6 93.2 %while.45 = (s32[]{:T(128)}, f32[4,512]{1,0:T(4,128)S(1)}, s32[4,4,64]{2,1,0:T(4,128)S(1)}, bf16[128,6272]{1,0:T(8,128)(2,1)}, f32[4,3,512]{2,1,0:T(4,128)S(1)},...) while((s32[]{:T(128)}, f32[4,512]{1,0:T(4,128)S(1)}, ...), condition=%wide.region_11.12_spmd.clone, body=%wide.region_8.11_spmd.clone.sunk | while | flops 861898496 | bytes 92647080 | solution.py:248
  425.9 2.7 copy-done.2
  429.6 3.1 reshape.996
  432.7 6.9 %fusion.129 = f32[4,64,49,128]{3,2,1,0:T(8,128)S(1)} fusion(bf16[4,64,49,128]{3,2,1,0:T(8,128)(2,1)} %reshape.996, f32[128]{0:T(128)S(1)} %multiply_bitcast_fusion.4, f32[128]{0:T(128)S(1)} %multiply_add_fusion.29, f32[4,64,128]{2,1,0:T(8,128)S(1)} %add_sqrt_fusion.6), kind=kOutput, calls=%fused_computation.17.clone.1 | convolution fusion | flops 432013312 | bytes 9765888 | tf_op jit(solution)/shard_map/while/body/eval_jaxpr/bjik,bjkp->bjip/dot_general | solution.py:115
  439.6 4.3 fusion.130
  452.9 3.1 reshape.996
  456.0 6.9 %fusion.129 = f32[4,64,49,128]{3,2,1,0:T(8,128)S(1)} fusion(bf16[4,64,49,128]{3,2,1,0:T(8,128)(2,1)} %reshape.996, f32[128]{0:T(128)S(1)} %multiply_bitcast_fusion.4, f32[128]{0:T(128)S(1)} %multiply_add_fusion.29, f32[4,64,128]{2,1,0:T(8,128)S(1)} %add_sqrt_fusion.6), kind=kOutput, calls=%fused_computation.17.clone.1 | convolution fusion | flops 432013312 | bytes 9765888 | tf_op jit(solution)/shard_map/while/body/eval_jaxpr/bjik,bjkp->bjip/dot_general | solution.py:115
  462.9 4.3 fusion.130
  476.2 3.1 reshape.996
  479.3 6.9 %fusion.129 = f32[4,64,49,128]{3,2,1,0:T(8,128)S(1)} fusion(bf16[4,64,49,128]{3,2,1,0:T(8,128)(2,1)} %reshape.996, f32[128]{0:T(128)S(1)} %multiply_bitcast_fusion.4, f32[128]{0:T(128)S(1)} %multiply_add_fusion.29, f32[4,64,128]{2,1,0:T(8,128)S(1)} %add_sqrt_fusion.6), kind=kOutput, calls=%fused_computation.17.clone.1 | convolution fusion | flops 432013312 | bytes 9765888 | tf_op jit(solution)/shard_map/while/body/eval_jaxpr/bjik,bjkp->bjip/dot_general | solution.py:115
  486.2 4.3 fusion.130
  499.5 3.1 reshape.996
  502.6 6.9 %fusion.129 = f32[4,64,49,128]{3,2,1,0:T(8,128)S(1)} fusion(bf16[4,64,49,128]{3,2,1,0:T(8,128)(2,1)} %reshape.996, f32[128]{0:T(128)S(1)} %multiply_bitcast_fusion.4, f32[128]{0:T(128)S(1)} %multiply_add_fusion.29, f32[4,64,128]{2,1,0:T(8,128)S(1)} %add_sqrt_fusion.6), kind=kOutput, calls=%fused_computation.17.clone.1 | convolution fusion | flops 432013312 | bytes 9765888 | tf_op jit(solution)/shard_map/while/body/eval_jaxpr/bjik,bjkp->bjip/dot_general | solution.py:115
  509.5 4.3 fusion.130
  (810 shorter events, 154.6 us)
Async XLA Ops:
  0.0 283.8 %copy-start = (f32[3,128]{1,0:T(4,128)S(1)}, f32[3,128]{1,0:T(4,128)}, u32[]{:S(2)}) copy-start(f32[3,128]{1,0:T(4,128)} %param.25) | copy-start | bytes 4612
  0.3 91.8 %copy-start.18 = (s32[128]{0:T(128)}, s32[128]{0:T(128)S(1)}, u32[]{:S(2)}) copy-start(s32[128]{0:T(128)S(1)} %reduce) | copy-start | bytes 1540
  1.5 90.8 %copy-start.4 = (f32[3,2048]{1,0:T(4,128)S(1)}, f32[3,2048]{1,0:T(4,128)}, u32[]{:S(2)}) copy-start(f32[3,2048]{1,0:T(4,128)} %param.22) | copy-start | bytes 73732
  1.5 92.2 %copy-start.21 = (f32[128]{0:T(128)S(1)}, f32[128]{0:T(128)}, u32[]{:S(2)}) copy-start(f32[128]{0:T(128)} %param.23) | copy-start | bytes 1540
  1.5 92.8 %copy-start.15 = (s32[2048]{0:T(1024)S(1)}, s32[2048]{0:T(1024)}, u32[]{:S(2)}) copy-start(s32[2048]{0:T(1024)} %param.19) | copy-start | bytes 24580
  1.6 92.8 %copy-start.16 = (f32[2048]{0:T(1024)S(1)}, f32[2048]{0:T(1024)}, u32[]{:S(2)}) copy-start(f32[2048]{0:T(1024)} %param.18) | copy-start | bytes 24580
  92.1 4.0 copy-start.9
  96.1 0.6 copy-start.13
  103.2 0.6 copy-start.11
  114.3 2.8 copy-start.14
  117.1 0.6 copy-start.13
  124.2 0.6 copy-start.11
  135.2 2.8 copy-start.14
  138.0 0.6 copy-start.13
  145.1 0.6 copy-start.11
  156.1 2.8 copy-start.14
  158.9 0.6 copy-start.13
  166.0 0.6 copy-start.11
  177.1 2.8 copy-start.14
  183.2 18.8 %copy-start.10 = (s32[16384]{0:T(1024)S(1)}, s32[16384]{0:T(1024)}, u32[]{:S(2)}) copy-start(s32[16384]{0:T(1024)} %copy-done.9) | copy-start | bytes 196612
  183.2 19.4 %copy-start.12 = (s32[16,64]{1,0:T(8,128)S(1)}, s32[16,64]{1,0:T(8,128)}, u32[]{:S(2)}) copy-start(s32[16,64]{1,0:T(8,128)} %param.20) | copy-start | bytes 12292
  183.2 19.5 %copy-start.20 = (s32[9]{0:T(128)S(1)}, s32[9]{0:T(128)}, u32[]{:S(2)}) copy-start(s32[9]{0:T(128)} %constant.1017) | copy-start | bytes 112
  190.3 19.1 %copy-start.19 = (s32[128]{0:T(128)S(1)}, s32[128]{0:T(128)}, u32[]{:S(2)}) copy-start(s32[128]{0:T(128)} %copy-done.18) | copy-start | bytes 1540
  190.3 19.7 %copy-start.8 = (s32[16384]{0:T(1024)S(1)}, s32[16384]{0:T(1024)}, u32[]{:S(2)}) copy-start(s32[16384]{0:T(1024)} %param.21) | copy-start | bytes 196612
  190.3 94.1 %all-to-all-start = ((bf16[128,2,6272]{2,1,0:T(2,128)(2,1)}), bf16[128,2,6272]{2,1,0:T(2,128)(2,1)}, u32[]{:S(2)}, u32[]{:S(2)}) async-start(bf16[128,2,6272]{2,1,0:T(2,128)(2,1)} %all_to_all.19), calls=%async_computation | async-start | bytes 6422528 | tf_op jit(solution)/shard_map/all_to_all | solution.py:219
  304.9 0.7 copy-start.7
  306.9 19.9 %all-to-all-start.2 = ((f32[128,1,288]{2,1,0:T(1,128)}), f32[128,1,288]{2,1,0:T(1,128)S(1)}, u32[]{:S(2)}, u32[]{:S(2)}) async-start(f32[128,1,288]{2,1,0:T(1,128)} %reshape.983), calls=%async_computation.2 | async-start | bytes 393216 | tf_op jit(solution)/shard_map/all_to_all | solution.py:229
  321.4 20.8 %copy-start.6 = (f32[4,3,512]{2,1,0:T(4,128)S(1)}, f32[4,3,512]{2,1,0:T(4,128)}, u32[]{:S(2)}) copy-start(f32[4,3,512]{2,1,0:T(4,128)} %get-tuple-element.1390) | copy-start | bytes 73732
  326.8 6.0 %copy-start.5 = (f32[128,1,288]{2,1,0:T(1,128)}, f32[128,1,288]{2,1,0:T(1,128)S(1)}, u32[]{:S(2)}) copy-start(f32[128,1,288]{2,1,0:T(1,128)S(1)} %all-to-all-done.2) | copy-start | bytes 442372
  326.8 85.7 %all-to-all-start.1 = ((bf16[128,2,6272]{2,1,0:T(2,128)(2,1)}), bf16[128,2,6272]{2,1,0:T(2,128)(2,1)}, u32[]{:S(2)}, u32[]{:S(2)}) async-start(bf16[128,2,6272]{2,1,0:T(2,128)(2,1)} %all_to_all.22), calls=%async_computation.1 | async-start | bytes 6422528 | tf_op jit(solution)/shard_map/all_to_all | solution.py:227
  412.5 6.3 %copy-start.17 = (s32[128]{0:T(128)S(1)}, s32[128]{0:T(128)}, u32[]{:S(2)}) copy-start(s32[128]{0:T(128)} %get-tuple-element.973) | copy-start | bytes 1540
  412.5 8.1 %copy-start.22 = (f32[1,1,128,1]{2,3,1,0:T(1,128)S(1)}, f32[1,1,128,1]{2,3,1,0:T(1,128)}, u32[]{:S(2)}) copy-start(f32[1,1,128,1]{2,3,1,0:T(1,128)} %get-tuple-element.1340) | copy-start | bytes 1540
  424.2 4.3 copy-start.3
  425.8 2.7 copy-start.2
  447.5 4.3 copy-start.3
  449.1 2.7 copy-start.2
  470.8 4.3 copy-start.3
  472.4 2.7 copy-start.2
  494.1 4.3 copy-start.3
  495.7 2.7 copy-start.2
  513.8 0.7 copy-start.1
